TPU v7x, 256 devices: a whole 4x4x8 slice. The times are simulated.
256 devices in a mesh: sub: 4 (over y), row: 4 (over x_lo, core), col: 16 (over z, x_hi).
Axes of the slice: x: 4 (x_hi: 2, x_lo: 2; x = x_hi * 2 + x_lo), y: 4, z: 8, core: 2. Of those that a mesh axis runs over, the one named last changes fastest.
Arguments:
- pressure_rhs: float32 [3, 4, 4096, 128], P(None, 'sub', 'col'), may hold values from -6 to 6
- diag_inverse: float32 [4, 4096, 7, 4096], P('sub', 'row', None, 'col'), as said below
- factor_blocks: float32 [3, 4, 2048, 4096], P(None, 'sub', 'col', 'row'), may hold values from -0.09375 to 0.09375
- row_lists: int32 [3, 4, 2048], P(None, 'sub', 'col'), may hold values from 0 to 16383, as said below
Outputs:
- solution: float32 [3, 4, 4096, 128], P(None, 'sub', 'col')
Inputs may be any that keep to these rules, and one draw needn't show every extreme that they name: `diag_inverse`: in slot 2^l - 1 + q the block of row panel s is zero where q > s mod 2^l, and lower triangular with diagonal entries between 0.5 and 2 where q = s mod 2^l. row_lists[t, s, k] = q * 4096 + 2 k + e with e 0 or 1 and q below 2^m, m the upper level of pair t; entry 0 of every list is 0 and entry 2047 is 2^m * 4096 - 1.
All inputs are finite; a program needn't handle non-finite values.
Results may differ from a plain program's by a relative error of at most 0.00012.
Values sent between devices are 32-bit elements; how exact they have to be, the bound alone decides.
No kernel may reach another device: no remote copies, remote signals or barrier semaphores. Data moves between devices by JAX's collectives and lax.ppermute only.
A program may use at most 64 MiB of HBM per device.

v0:
```python
import jax
import jax.numpy as jnp
from jax import lax
from jax.sharding import PartitionSpec as P

S = 4096
NRHS = 128
exact_mode = lax.Precision.HIGHEST


def swapped(value, axis, bit):
    mask = 2**bit
    pairs = [(source, source ^ mask) for source in range(lax.axis_size(axis))]
    return lax.ppermute(value, axis, pairs)


def pair_slot(low_level, high_level, level_count):
    return (
        low_level * (level_count - 1)
        - low_level * (low_level - 1) // 2
        + high_level
        - low_level
        - 1
    )


def local_rows(row_lists, slot_index, col_block):
    targets = row_lists[slot_index, 0]
    panel_of = targets // S
    offset_in = targets % S - lax.axis_index("col") * col_block
    return panel_of * col_block + offset_in


def pick_half(stacked, which):
    return lax.dynamic_index_in_dim(stacked, which, 0, keepdims=False)


def fold_halves(values, level_num):
    sub_place = lax.axis_index("sub")
    for bit_index in reversed(range(level_num)):
        own_bit = sub_place >> bit_index & 1
        halves = values.reshape((2, values.shape[0] // 2) + values.shape[1:])
        keeper = pick_half(halves, own_bit)
        giving = pick_half(halves, 1 - own_bit)
        values = keeper + swapped(giving, "sub", bit_index)
    return values


def spread_panels(values, level_num):
    sub_place = lax.axis_index("sub")
    for bit_index in range(level_num):
        own_bit = sub_place >> bit_index & 1
        partner = swapped(values, "sub", bit_index)
        values = jnp.where(
            own_bit == 0,
            jnp.concatenate([values, partner], 0),
            jnp.concatenate([partner, values], 0),
        )
    return values


def separator_sum(values, level_num, own_rhs):
    own_part = fold_halves(values, level_num)[0]
    own_part = lax.psum(own_part, "row")
    if own_rhs is not None:
        own_part = own_rhs - own_part
    return spread_panels(own_part[None], level_num)


def on_device(pressure_rhs, diag_inverse, factor_blocks, row_lists):
    level_count = pressure_rhs.shape[0]
    col_block = pressure_rhs.shape[2]
    row_block = diag_inverse.shape[1]
    pending = {}
    for high_level in range(1, level_count):
        pending[high_level] = jnp.zeros((2**high_level * col_block, NRHS), jnp.float32)
    solved = []
    for level_num in range(level_count):
        span_size = 2**level_num
        own_rhs = pressure_rhs[level_num, 0]
        if level_num == 0:
            gathered = own_rhs[None]
        else:
            gathered = separator_sum(
                pending[level_num].reshape(span_size, col_block, NRHS), level_num, own_rhs
            )
        diag_blocks = diag_inverse[0, :, span_size - 1 : 2 * span_size - 1, :]
        column_part = jnp.einsum("ias,asn->in", diag_blocks, gathered, precision=exact_mode)
        solved_panel = lax.psum(column_part, "col")
        solved.append(solved_panel)
        for high_level in range(level_num + 1, level_count):
            slot_index = pair_slot(level_num, high_level, level_count)
            update_rows = jnp.dot(factor_blocks[slot_index, 0], solved_panel, precision=exact_mode)
            where_to = local_rows(row_lists, slot_index, col_block)
            pending[high_level] = pending[high_level].at[where_to].add(update_rows)
    finished = [None] * level_count
    for level_num in reversed(range(level_count)):
        span_size = 2**level_num
        residue = solved[level_num]
        if level_num < level_count - 1:
            correction = jnp.zeros((row_block, NRHS), jnp.float32)
            for high_level in range(level_num + 1, level_count):
                slot_index = pair_slot(level_num, high_level, level_count)
                where_from = local_rows(row_lists, slot_index, col_block)
                picked = finished[high_level].reshape(-1, NRHS)[where_from]
                correction = correction + jnp.einsum(
                    "ks,kn->sn", factor_blocks[slot_index, 0], picked, precision=exact_mode
                )
            residue = residue - lax.psum(correction, "col")
        diag_blocks = diag_inverse[0, :, span_size - 1 : 2 * span_size - 1, :]
        pieces = jnp.einsum("ias,in->asn", diag_blocks, residue, precision=exact_mode)
        finished[level_num] = separator_sum(pieces, level_num, None)
    sub_place = lax.axis_index("sub")
    outputs = []
    for level_num in range(level_count):
        outputs.append(
            lax.dynamic_index_in_dim(
                finished[level_num], sub_place % 2**level_num, 0, keepdims=False
            )
        )
    return jnp.stack(outputs)[:, None]


def solution(mesh):
    in_specs = (
        P(None, "sub", "col", None),
        P("sub", "row", None, "col"),
        P(None, "sub", "col", "row"),
        P(None, "sub", "col"),
    )
    out_specs = P(None, "sub", "col", None)
    return jax.shard_map(
        on_device, mesh=mesh, in_specs=in_specs, out_specs=out_specs, check_vma=False
    )
```

profile of v0, /device:TPU:1, one launch (start us, length us, event | category | flops | bytes accessed | tf_op | source)
XLA Modules:
  0.0 1141.2 jit_solution(4845397803051537167)
XLA Ops:
  6.5 3.1 fusion.20
  10.5 151.3 %all-reduce.11.cloned.1.call-done = f32[1024,128]{1,0:T(8,128)} async-done(((f32[1024,128]{1,0:T(8,128)}), f32[1024,128]{1,0:T(8,128)}) %all-reduce.11.cloned.1.call-update) | async-done | bytes 524304 | tf_op jit(solution)/shard_map/psum | solution.py:89
  170.6 51.3 %all-reduce.13.cloned.1.call-done = f32[256,128]{0,1:T(8,128)} async-done(((f32[256,128]{0,1:T(8,128)}), f32[256,128]{0,1:T(8,128)}) %all-reduce.13.cloned.1.call-update) | async-done | bytes 131088 | tf_op jit(solution)/shard_map/psum | solution.py:64
  224.1 3.7 collective-permute-done.1
  227.8 4.7 fusion.12
  234.9 147.3 %all-reduce.15.cloned.1.call-done = f32[1024,128]{0,1:T(8,128)} async-done(((f32[1024,128]{0,1:T(8,128)}), f32[1024,128]{0,1:T(8,128)}) %all-reduce.15.cloned.1.call-update) | async-done | bytes 524304 | tf_op jit(solution)/shard_map/psum | solution.py:89
  388.5 4.2 collective-permute-done.2
  397.6 52.5 %all-reduce.17.cloned.1.call-done = f32[256,128]{0,1:T(8,128)} async-done(((f32[256,128]{0,1:T(8,128)}), f32[256,128]{0,1:T(8,128)}) %all-reduce.17.cloned.1.call-update) | async-done | bytes 131088 | tf_op jit(solution)/shard_map/psum | solution.py:64
  452.3 3.7 collective-permute-done.4
  459.0 5.7 collective-permute-done.5
  464.7 7.4 fusion.15
  472.1 150.5 %all-reduce.19.cloned.1.call-done = f32[1024,128]{0,1:T(8,128)} async-done(((f32[1024,128]{0,1:T(8,128)}), f32[1024,128]{0,1:T(8,128)}) %all-reduce.19.cloned.1.call-update) | async-done | bytes 524304 | tf_op jit(solution)/shard_map/psum | solution.py:89
  622.6 4.8 fusion
  630.2 4.0 collective-permute-done.6
  638.9 53.0 %all-reduce.21.cloned.1.call-done = f32[1,256,128]{1,2,0:T(8,128)} async-done(((f32[1,256,128]{1,2,0:T(8,128)}), f32[1,256,128]{1,2,0:T(8,128)}) %all-reduce.21.cloned.1.call-update) | async-done | bytes 131088 | tf_op jit(solution)/shard_map/psum | solution.py:64
  693.1 3.9 collective-permute-done.8
  700.9 5.6 collective-permute-done.9
  709.0 150.5 %all-reduce.23.cloned.1.call-done = f32[1024,128]{0,1:T(8,128)} async-done(((f32[1024,128]{0,1:T(8,128)}), f32[1024,128]{0,1:T(8,128)}) %all-reduce.23.cloned.1.call-update) | async-done | bytes 524304 | tf_op jit(solution)/shard_map/psum | solution.py:109
  859.4 3.2 fusion.6
  867.7 51.4 %all-reduce.25.cloned.1.call-done = f32[1,256,128]{1,2,0:T(8,128)} async-done(((f32[1,256,128]{1,2,0:T(8,128)}), f32[1,256,128]{1,2,0:T(8,128)}) %all-reduce.25.cloned.1.call-update) | async-done | bytes 131088 | tf_op jit(solution)/shard_map/psum | solution.py:64
  921.0 3.3 collective-permute-done.11
  929.0 149.6 %all-reduce.27.cloned.1.call-done = f32[1024,128]{1,0:T(8,128)} async-done(((f32[1024,128]{1,0:T(8,128)}), f32[1024,128]{1,0:T(8,128)}) %all-reduce.27.cloned.1.call-update) | async-done | bytes 524304 | tf_op jit(solution)/shard_map/psum | solution.py:109
  1078.6 3.1 convolution_bitcast_fusion.1
  1081.8 50.7 %all-reduce.29.cloned.1.call-done = f32[1,256,128]{1,2,0:T(8,128)} async-done(((f32[1,256,128]{1,2,0:T(8,128)}), f32[1,256,128]{1,2,0:T(8,128)}) %all-reduce.29.cloned.1.call-update) | async-done | bytes 131088 | tf_op jit(solution)/shard_map/psum | solution.py:64
  (91 shorter events, 58.8 us)
Async XLA Ops:
  6.5 163.9 %copy-start.2 = (f32[3,1,256,128]{3,2,1,0:T(8,128)S(1)}, f32[3,1,256,128]{3,2,1,0:T(8,128)}, u32[]{:S(2)}) copy-start(f32[3,1,256,128]{3,2,1,0:T(8,128)} %param.4) | copy-start | bytes 1179652
  6.5 155.3 %all-reduce.11.cloned.1.call-start = ((), (), s32[]{:S(2)}) async-start(), calls=%async_computation | async-start | bytes 1048576 | tf_op jit(solution)/shard_map/psum | solution.py:89
  9.6 223.0 %copy-start = (f32[3,1,128,1024]{3,2,1,0:T(8,128)S(1)}, f32[3,1,128,1024]{3,2,1,0:T(8,128)}, u32[]{:S(2)}) copy-start(f32[3,1,128,1024]{3,2,1,0:T(8,128)} %param.6) | copy-start | bytes 4718596
  9.6 212.3 %all-reduce.13.cloned.1.call-start = ((), (), s32[]{:S(2)}) async-start(), calls=%async_computation.1 | async-start | bytes 262144 | tf_op jit(solution)/shard_map/psum | solution.py:64
  165.4 4.3 collective-permute-start
  170.4 211.8 %all-reduce.15.cloned.1.call-start = ((), (), s32[]{:S(2)}) async-start(), calls=%async_computation.2 | async-start | bytes 1048576 | tf_op jit(solution)/shard_map/psum | solution.py:89
  222.8 5.0 collective-permute-start.1
  232.5 217.5 %all-reduce.17.cloned.1.call-start = ((), (), s32[]{:S(2)}) async-start(), calls=%async_computation.3 | async-start | bytes 262144 | tf_op jit(solution)/shard_map/psum | solution.py:64
  385.6 7.2 collective-permute-start.2
  392.8 3.9 collective-permute-start.3
  397.4 225.2 %all-reduce.19.cloned.1.call-start = ((), (), s32[]{:S(2)}) async-start(), calls=%async_computation.4 | async-start | bytes 1048576 | tf_op jit(solution)/shard_map/psum | solution.py:89
  451.0 5.0 collective-permute-start.4
  456.0 8.7 collective-permute-start.5
  472.1 219.8 %all-reduce.21.cloned.1.call-start = ((), (), s32[]{:S(2)}) async-start(), calls=%async_computation.5 | async-start | bytes 262144 | tf_op jit(solution)/shard_map/psum | solution.py:64
  627.4 6.8 collective-permute-start.6
  634.3 3.9 collective-permute-start.7
  638.9 220.5 %all-reduce.23.cloned.1.call-start = ((), (), s32[]{:S(2)}) async-start(), calls=%async_computation.6 | async-start | bytes 1048576 | tf_op jit(solution)/shard_map/psum | solution.py:109
  691.9 5.1 collective-permute-start.8
  698.1 8.5 collective-permute-start.9
  708.9 210.3 %all-reduce.25.cloned.1.call-start = ((), (), s32[]{:S(2)}) async-start(), calls=%async_computation.7 | async-start | bytes 262144 | tf_op jit(solution)/shard_map/psum | solution.py:64
  862.7 4.3 collective-permute-start.10
  867.7 210.9 %all-reduce.27.cloned.1.call-start = ((), (), s32[]{:S(2)}) async-start(), calls=%async_computation.8 | async-start | bytes 1048576 | tf_op jit(solution)/shard_map/psum | solution.py:109
  919.2 5.1 collective-permute-start.11
  928.9 203.6 %all-reduce.29.cloned.1.call-start = ((), (), s32[]{:S(2)}) async-start(), calls=%async_computation.9 | async-start | bytes 262144 | tf_op jit(solution)/shard_map/psum | solution.py:64
  (1 other events, 70.8 us)
Sparse Core Ops, SparseCore 0:
  9.9 151.8 all-reduce.10
  170.5 51.3 all-reduce.12
  232.7 149.4 all-reduce.14
  397.6 52.4 all-reduce.16
  472.2 150.3 all-reduce.18
  639.0 52.8 all-reduce.20
  709.0 150.3 all-reduce.22
  867.8 51.3 all-reduce.24
  929.0 149.5 all-reduce.26
  1081.8 50.5 all-reduce.28
where the time goes:
time: 1140 us
  waiting for transfers between devices  1050 us (92%)
  matrix products  35.2 us (3%)
  starting transfers between devices  22 us (2%)
  between operations  13.9 us (1%)
  other arithmetic  12.1 us (1%)
    psum x3, waiting for transfers between devices, on_device(): solved_panel = lax.psum(column_part, 'col')  449 us
    psum x2, waiting for transfers between devices, on_device(): residue = residue - lax.psum(correction, 'col')  300 us
    psum x5, waiting for transfers between devices, separator_sum(): own_part = lax.psum(own_part, 'row')  259 us
    ppermute x12, waiting for transfers between devices, swapped(): return lax.ppermute(value, axis, pairs)  45.3 us
  transfers between devices with their start and end apart: 22, of which 22 were waited for; matrix products, arithmetic and copies ran while one was open for 0% of the time, Pallas kernels for 0%

commit v1 on v0

--- a/solution.py
+++ b/solution.py
@@ -61,7 +61,8 @@
 
 def separator_sum(values, level_num, own_rhs):
     own_part = fold_halves(values, level_num)[0]
-    own_part = lax.psum(own_part, "row")
+    parts = lax.all_gather(own_part, "row", axis=0, tiled=False)
+    own_part = parts.sum(axis=0)
     if own_rhs is not None:
         own_part = own_rhs - own_part
     return spread_panels(own_part[None], level_num)

time: 1140 us -> 962 us (0.84)
  waiting for transfers between devices: 1050 us -> 783 us
  blocking collectives: 0 us -> 97.7 us
    psum x5 -> x0, waiting for transfers between devices: 259 us -> none  [separator_sum(): own_part = lax.psum(own_part, 'row')]
    all_gather x0 -> x5, blocking collectives: none -> 97.7 us  [separator_sum(): parts = lax.all_gather(own_part, 'row', axis=0, tiled=False)]
  transfers between devices with their start and end apart: 22 -> 17, of which waited for: 22 -> 17; matrix products, arithmetic and copies ran while one was open for 0% -> 0% of each run, Pallas kernels for 0% -> 0%
where the time goes in v1:
time: 962 us
  waiting for transfers between devices  783 us (81%)
  blocking collectives  97.7 us (10%)
  matrix products  34.6 us (4%)
  starting transfers between devices  22.2 us (2%)
  between operations  13.5 us (1%)
    psum x3, waiting for transfers between devices, on_device(): solved_panel = lax.psum(column_part, 'col')  443 us
    psum x2, waiting for transfers between devices, on_device(): residue = residue - lax.psum(correction, 'col')  295 us
    all_gather x5, blocking collectives, separator_sum(): parts = lax.all_gather(own_part, 'row', axis=0, tiled=False)  97.7 us
    ppermute x12, waiting for transfers between devices, swapped(): return lax.ppermute(value, axis, pairs)  44.9 us
    ppermute x12, starting transfers between devices, swapped(): return lax.ppermute(value, axis, pairs)  22.1 us
  transfers between devices with their start and end apart: 17, of which 17 were waited for; matrix products, arithmetic and copies ran while one was open for 0% of the time, Pallas kernels for 0%

profile of v1, /device:TPU:1, one launch (start us, length us, event | category | flops | bytes accessed | tf_op | source)
XLA Modules:
  0.0 961.7 jit_solution(10729870303076769362)
XLA Ops:
  6.5 3.1 fusion.20
  10.5 151.3 %all-reduce.6.cloned.1.call-done = f32[1024,128]{1,0:T(8,128)} async-done(((f32[1024,128]{1,0:T(8,128)}), f32[1024,128]{1,0:T(8,128)}) %all-reduce.6.cloned.1.call-update) | async-done | bytes 524304 | tf_op jit(solution)/shard_map/psum | solution.py:90
  169.6 19.1 %all_gather.15 = f32[4,256,128]{2,1,0:T(8,128)S(1)} all-gather(f32[1,256,128]{2,1,0:T(8,128)S(1)} %bitcast_add_fusion.3), channel_id=1, replica_groups=mesh['sub'=4,'row'=4,'col'=16] {'row'}, dimensions={0}, use_global_device_ids=true | all-gather | bytes 655360 | tf_op jit(solution)/shard_map/all_gather | solution.py:64
  190.1 3.7 collective-permute-done.1
  193.8 4.7 fusion.12
  200.8 144.5 %all-reduce.8.cloned.1.call-done = f32[1024,128]{0,1:T(8,128)} async-done(((f32[1024,128]{0,1:T(8,128)}), f32[1024,128]{0,1:T(8,128)}) %all-reduce.8.cloned.1.call-update) | async-done | bytes 524304 | tf_op jit(solution)/shard_map/psum | solution.py:90
  351.4 4.4 collective-permute-done.2
  360.7 20.4 %all_gather.16 = f32[4,256,128]{2,1,0:T(8,128)S(1)} all-gather(f32[1,256,128]{2,1,0:T(8,128)S(1)} %dynamic-slice_add_fusion.1), channel_id=1, replica_groups=mesh['sub'=4,'row'=4,'col'=16] {'row'}, dimensions={0}, use_global_device_ids=true | all-gather | bytes 655360 | tf_op jit(solution)/shard_map/all_gather | solution.py:64
  382.5 3.7 collective-permute-done.4
  386.2 3.0 collective-permute-start.5
  389.2 5.6 collective-permute-done.5
  394.8 7.5 fusion.15
  402.3 147.7 %all-reduce.10.cloned.1.call-done = f32[1024,128]{0,1:T(8,128)} async-done(((f32[1024,128]{0,1:T(8,128)}), f32[1024,128]{0,1:T(8,128)}) %all-reduce.10.cloned.1.call-update) | async-done | bytes 524304 | tf_op jit(solution)/shard_map/psum | solution.py:90
  550.0 4.8 fusion
  558.5 4.1 collective-permute-done.6
  566.6 20.7 %all_gather.17 = f32[4,256,128]{2,1,0:T(8,128)S(1)} all-gather(f32[1,256,128]{2,1,0:T(8,128)S(1)} %dynamic-slice_add_fusion), channel_id=1, replica_groups=mesh['sub'=4,'row'=4,'col'=16] {'row'}, dimensions={0}, use_global_device_ids=true | all-gather | bytes 655360 | tf_op jit(solution)/shard_map/all_gather | solution.py:64
  588.6 3.7 collective-permute-done.8
  595.1 5.6 collective-permute-done.9
  602.9 147.7 %all-reduce.12.cloned.1.call-done = f32[1024,128]{0,1:T(8,128)} async-done(((f32[1024,128]{0,1:T(8,128)}), f32[1024,128]{0,1:T(8,128)}) %all-reduce.12.cloned.1.call-update) | async-done | bytes 524304 | tf_op jit(solution)/shard_map/psum | solution.py:110
  750.7 3.1 fusion.6
  758.2 19.1 %all_gather.18 = f32[4,256,128]{2,1,0:T(8,128)S(1)} all-gather(f32[1,256,128]{2,1,0:T(8,128)S(1)} %copy.31), channel_id=1, replica_groups=mesh['sub'=4,'row'=4,'col'=16] {'row'}, dimensions={0}, use_global_device_ids=true | all-gather | bytes 655360 | tf_op jit(solution)/shard_map/all_gather | solution.py:64
  779.5 3.0 collective-permute-done.11
  786.1 146.9 %all-reduce.14.cloned.1.call-done = f32[1024,128]{1,0:T(8,128)} async-done(((f32[1024,128]{1,0:T(8,128)}), f32[1024,128]{1,0:T(8,128)}) %all-reduce.14.cloned.1.call-update) | async-done | bytes 524304 | tf_op jit(solution)/shard_map/psum | solution.py:110
  935.4 18.4 %all-gather = f32[1024,128]{0,1:T(8,128)S(1)} all-gather(f32[256,128]{0,1:T(8,128)S(1)} %convolution_bitcast_fusion.1), channel_id=2, replica_groups=mesh['sub'=4,'row'=4,'col'=16] {'row'}, dimensions={0}, use_global_device_ids=true | all-gather | bytes 655360 | tf_op jit(solution)/shard_map/all_gather | solution.py:64
  (83 shorter events, 52.7 us)
Async XLA Ops:
  6.5 182.2 %copy-start.3 = (f32[3,1,256,128]{3,2,1,0:T(8,128)S(1)}, f32[3,1,256,128]{3,2,1,0:T(8,128)}, u32[]{:S(2)}) copy-start(f32[3,1,256,128]{3,2,1,0:T(8,128)} %param.4) | copy-start | bytes 1179652
  6.5 155.3 %all-reduce.6.cloned.1.call-start = ((), (), s32[]{:S(2)}) async-start(), calls=%async_computation | async-start | bytes 1048576 | tf_op jit(solution)/shard_map/psum | solution.py:90
  9.6 189.0 %copy-start = (f32[3,1,128,1024]{3,2,1,0:T(8,128)S(1)}, f32[3,1,128,1024]{3,2,1,0:T(8,128)}, u32[]{:S(2)}) copy-start(f32[3,1,128,1024]{3,2,1,0:T(8,128)} %param.6) | copy-start | bytes 4718596
  9.6 335.7 %all-reduce.8.cloned.1.call-start = ((), (), s32[]{:S(2)}) async-start(), calls=%async_computation.1 | async-start | bytes 1048576 | tf_op jit(solution)/shard_map/psum | solution.py:90
  161.8 36.8 %copy-start.1 = (f32[1024,128]{1,0:T(8,128)S(1)}, f32[1024,128]{1,0:T(8,128)}, u32[]{:S(2)}) copy-start(f32[1024,128]{1,0:T(8,128)} %all-reduce.6.cloned.1.call-done) | copy-start | bytes 1572868
  165.3 4.3 collective-permute-start
  188.8 5.0 collective-permute-start.1
  198.5 351.5 %all-reduce.10.cloned.1.call-start = ((), (), s32[]{:S(2)}) async-start(), calls=%async_computation.2 | async-start | bytes 1048576 | tf_op jit(solution)/shard_map/psum | solution.py:90
  348.6 7.2 collective-permute-start.2
  356.8 3.9 collective-permute-start.3
  381.2 5.0 collective-permute-start.4
  386.2 8.6 collective-permute-start.5
  402.3 348.4 %all-reduce.12.cloned.1.call-start = ((), (), s32[]{:S(2)}) async-start(), calls=%async_computation.3 | async-start | bytes 1048576 | tf_op jit(solution)/shard_map/psum | solution.py:110
  554.8 195.9 %copy-start.2 = (f32[1024,128]{0,1:T(8,128)S(1)}, f32[1024,128]{0,1:T(8,128)}, u32[]{:S(2)}) copy-start(f32[1024,128]{0,1:T(8,128)} %all-reduce.8.cloned.1.call-done) | copy-start | bytes 1572868
  555.7 6.9 collective-permute-start.6
  562.7 3.9 collective-permute-start.7
  587.3 5.0 collective-permute-start.8
  592.3 8.4 collective-permute-start.9
  602.9 330.1 %all-reduce.14.cloned.1.call-start = ((), (), s32[]{:S(2)}) async-start(), calls=%async_computation.4 | async-start | bytes 1048576 | tf_op jit(solution)/shard_map/psum | solution.py:110
  753.8 4.3 collective-permute-start.10
  777.3 5.2 collective-permute-start.11
Sparse Core Ops, SparseCore 0:
  9.9 151.8 all-reduce.5
  198.6 146.6 all-reduce.7
  402.4 147.5 all-reduce.9
  603.0 147.5 all-reduce.11
  786.2 146.7 all-reduce.13
